TPU v7x, 32 devices: a whole 2x2x4 slice. The times are simulated.
32 devices in a mesh: ctx: 8 (over z, y), fsdp: 4 (over x, core).
Axes of the slice: x: 2, y: 2, z: 4, core: 2. Of those that a mesh axis runs over, the one named last changes fastest.
Arguments:
- tokens: bfloat16 [2048, 4096], P('ctx', 'fsdp'), may hold values from -150 to 150
- norm_gain: float32 [4096], replicated, may hold values from 0.1 to 1.9
- in_weight: bfloat16 [4096, 3, 4096], P('ctx', None, 'fsdp'), may hold values from -0.09375 to 0.09375
- short_filter: float32 [3, 3, 4096], P(None, None, 'fsdp'), may hold values from -3.5 to 3.5
- long_filter: bfloat16 [256, 128], P('fsdp'), may hold values from -0.5 to 0.5
- skip_gain: float32 [4096], P('fsdp'), may hold values from -4 to 4
- out_weight: bfloat16 [4096, 4096], P('fsdp', 'ctx'), may hold values from -0.09375 to 0.09375
Outputs:
- mixed: bfloat16 [2048, 4096], P('ctx', 'fsdp')
All inputs are finite; a program needn't handle non-finite values.
Results may differ from a plain program's by a relative error of at most 0.0091.
Values may be sent and summed in bfloat16 or wider, within the bound.
A program may use at most 128 MiB of HBM per device.

v0:
```python
import jax
import jax.numpy as jnp
from jax import lax
from jax.sharding import PartitionSpec as P


def passed_along(block, axis, distance):
    devices = range(lax.axis_size(axis))
    route = [(i - distance, i) for i in devices if i - distance in devices]
    return lax.ppermute(block, axis, route)


def toeplitz_blocks(long_filter, row_count):
    groups = long_filter.shape[0]
    flen = long_filter.shape[1]
    window = flen + row_count - 1
    reversed_taps = long_filter[:, ::-1]
    padded = jnp.concatenate(
        [reversed_taps, jnp.zeros((groups, row_count), long_filter.dtype)], axis=1
    )
    tiled = jnp.tile(padded, (1, row_count))
    return tiled[:, : row_count * window].reshape(groups, row_count, window)


def short_conv(taps, extended):
    return taps[0] * extended[2:] + taps[1] * extended[1:-1] + taps[2] * extended[:-2]


def on_device(tokens, norm_gain, in_weight, short_filter, long_filter, skip_gain, out_weight):
    whole = lax.all_gather(tokens, "fsdp", axis=1, tiled=True)
    row_count = whole.shape[0]
    values = whole.astype(jnp.float32)
    mean_square = jnp.mean(values * values, axis=-1, keepdims=True)
    normed = (values * lax.rsqrt(mean_square + 1e-06) * norm_gain).astype(jnp.bfloat16)
    share = in_weight.shape[2]
    width_all = 3 * share
    weight_rows = lax.all_gather(in_weight, "ctx", axis=0, tiled=True)
    flat_rows = weight_rows.reshape(weight_rows.shape[0], width_all)
    proj = jnp.dot(normed, flat_rows, preferred_element_type=jnp.float32).astype(jnp.bfloat16)
    taps = short_filter.reshape(3, width_all)
    flen = long_filter.shape[1]
    earlier = passed_along(proj[row_count - 2 :], "ctx", 1)
    extended = jnp.concatenate([earlier, proj], axis=0).astype(jnp.float32)
    filtered = short_conv(taps, extended)
    out_gate = filtered[:, :share]
    product = (filtered[:, share : 2 * share] * filtered[:, 2 * share :]).astype(jnp.bfloat16)
    previous = passed_along(product[row_count - (flen - 1) :], "ctx", 1)
    product_ext = jnp.concatenate([previous, product], axis=0)
    groups = long_filter.shape[0]
    group_width = share // groups
    window = row_count + flen - 1
    blocks = toeplitz_blocks(long_filter, row_count)
    conv = jnp.einsum(
        "gts,sgc->tgc",
        blocks,
        product_ext.reshape(window, groups, group_width),
        preferred_element_type=jnp.float32,
    ).reshape(row_count, share)
    gated = (out_gate * (conv + skip_gain * product.astype(jnp.float32))).astype(jnp.bfloat16)
    terms = jnp.dot(
        gated,
        lax.all_gather(out_weight, "ctx", axis=1, tiled=True),
        preferred_element_type=jnp.float32,
    )
    mixed = lax.psum_scatter(terms, "fsdp", scatter_dimension=1, tiled=True).astype(jnp.bfloat16)
    return mixed


def solution(mesh):
    in_specs = (
        P("ctx", "fsdp"),
        P(),
        P("ctx", None, "fsdp"),
        P(None, None, "fsdp"),
        P("fsdp", None),
        P("fsdp"),
        P("fsdp", "ctx"),
    )
    out_specs = P("ctx", "fsdp")
    return jax.shard_map(
        on_device, mesh=mesh, in_specs=in_specs, out_specs=out_specs, check_vma=False
    )
```

profile of v0, /device:TPU:0, one launch (start us, length us, event | category | flops | bytes accessed | tf_op | source)
XLA Modules:
  0.0 708.9 jit_solution(7502111385627137114)
XLA Ops:
  6.5 0.7 all-gather.4.cloned.1.call-update
  7.3 4.7 copy.10
  12.0 0.7 all-gather.8.cloned.1.call-update
  12.8 21.4 %all-gather.4.cloned.1.call-done = bf16[256,4096]{1,0:T(8,128)(2,1)} async-done(((bf16[256,1024]{1,0:T(8,128)(2,1)}), bf16[256,4096]{1,0:T(8,128)(2,1)}) %all-gather.4.cloned.1.call-update) | async-done | bytes 2097168 | tf_op jit(solution)/shard_map/all_gather | solution.py:30
  34.2 2.1 fusion
  36.3 479.9 %all-gather.6.cloned.1.call-done = bf16[4096,3,1024]{0,2,1:T(8,128)(2,1)} async-done(((bf16[512,3,1024]{0,2,1:T(8,128)(2,1)}), bf16[4096,3,1024]{0,2,1:T(8,128)(2,1)}) %all-gather.6.cloned.1.call-update) | async-done | bytes 25165840 | tf_op jit(solution)/shard_map/all_gather | solution.py:37
  516.2 12.2 %convolution_convert_fusion = bf16[256,3072]{1,0:T(8,128)(2,1)S(1)} fusion(bf16[4096,3072]{0,1:T(8,128)(2,1)} %bitcast.15, bf16[256,4096]{1,0:T(8,128)(2,1)} %all-gather.4.cloned.1.call-done, f32[4096]{0:T(1024)S(1)} %copy-done.4, f32[256]{0:T(256)S(1)} %add_rsqrt_fusion), kind=kOutput, calls=%fused_computation.5 | convolution fusion | flops 6447431680 | bytes 28853248 | tf_op jit(solution)/shard_map/dot_general | solution.py:39
  528.4 2.3 collective-permute-start
  530.8 1.5 collective-permute-done
  532.8 0.9 fusion.3
  533.9 0.8 copy-done
  534.7 5.1 collective-permute-start.1
  540.0 5.6 tile.4
  545.6 11.6 %copy.13 = bf16[8,8,256,384]{3,1,2,0:T(8,128)(2,1)S(1)} copy(bf16[8,8,256,384]{3,2,1,0:T(8,128)(2,1)} %bitcast.11) | data formatting | bytes 25165824
  557.2 5.2 slice.59
  562.5 34.2 %reshape.35 = bf16[64,256,383]{2,1,0:T(8,128)(2,1)} reshape(bf16[64,98048]{1,0:T(8,128)(2,1)} %slice.59) | data formatting | bytes 25100288 | tf_op jit(solution)/shard_map/reshape | solution.py:22
  596.7 2.2 pad_maximum_fusion
  598.9 2.3 copy.11
  601.2 9.3 %fusion.14 = f32[64,16,256]{2,1,0:T(8,128)} fusion(bf16[383,64,16]{0,2,1:T(8,128)(2,1)} %bitcast.14, bf16[64,256,383]{2,1,0:T(8,128)(2,1)} %reshape.35), kind=kOutput, calls=%fused_computation.23 | convolution fusion | flops 200802304 | bytes 14383104 | tf_op jit(solution)/shard_map/gts,sgc->tgc/dot_general | solution.py:53
  610.6 2.5 copy.12
  613.1 36.2 %all-gather.8.cloned.1.call-done = bf16[1024,4096]{1,0:T(8,128)(2,1)} async-done(((bf16[1024,512]{1,0:T(8,128)(2,1)}), bf16[1024,4096]{1,0:T(8,128)(2,1)}) %all-gather.8.cloned.1.call-update) | async-done | bytes 8388624 | tf_op jit(solution)/shard_map/all_gather | solution.py:62
  649.3 8.2 %fusion.10 = f32[256,4096]{1,0:T(8,128)} fusion(bf16[1024,4096]{1,0:T(8,128)(2,1)} %all-gather.8.cloned.1.call-done, f32[256,3072]{1,0:T(8,128)S(1)} %fusion.3, f32[256,1024]{1,0:T(8,128)} %copy.12, bf16[256,1024]{1,0:T(8,128)(2,1)} %copy-done, f32[1024]{0:T(1024)S(1)} %copy-done.1), kind=kOutput, calls=%fused_computation.19 | convolution fusion | flops 2148794368 | bytes 15208448 | tf_op jit(solution)/shard_map/dot_general | solution.py:60
  657.5 42.8 %reduce-scatter.2.cloned.1.call-done = f32[256,1024]{1,0:T(8,128)} async-done(((f32[256,4096]{1,0:T(8,128)}), f32[256,1024]{1,0:T(8,128)}) %reduce-scatter.2.cloned.1.call-update) | async-done | bytes 1048592 | tf_op jit(solution)/shard_map/reduce_scatter | solution.py:65
  700.3 2.1 convert_element_type.31
  (27 shorter events, 1.0 us)
Async XLA Ops:
  6.5 27.7 %all-gather.4.cloned.1.call-start = ((), (), s32[]{:S(2)}) async-start(), calls=%async_computation.1 | async-start | bytes 2621440 | tf_op jit(solution)/shard_map/all_gather | solution.py:30
  7.3 508.9 %all-gather.6.cloned.1.call-start = ((), (), s32[]{:S(2)}) async-start(), calls=%async_computation.2 | async-start | bytes 28311552 | tf_op jit(solution)/shard_map/all_gather | solution.py:37
  12.0 504.2 %copy-start.4 = (f32[4096]{0:T(1024)S(1)}, f32[4096]{0:T(1024)}, u32[]{:S(2)}) copy-start(f32[4096]{0:T(1024)} %param.8) | copy-start | bytes 49156
  12.0 637.3 %all-gather.8.cloned.1.call-start = ((), (), s32[]{:S(2)}) async-start(), calls=%async_computation.3 | async-start | bytes 9437184 | tf_op jit(solution)/shard_map/all_gather | solution.py:62
  12.7 687.5 %reduce-scatter.2.cloned.1.call-start = ((), (), s32[]{:S(2)}) async-start(), calls=%async_computation.4 | async-start | bytes 5242880 | tf_op jit(solution)/shard_map/reduce_scatter | solution.py:65
  516.2 14.6 %copy-start.2 = (f32[3,3,1024]{2,1,0:T(4,128)S(1)}, f32[3,3,1024]{2,1,0:T(4,128)}, u32[]{:S(2)}) copy-start(f32[3,3,1024]{2,1,0:T(4,128)} %param.10) | copy-start | bytes 110596
  528.4 3.9 collective-permute-start
  533.7 6.2 copy-start.3
  533.9 0.8 copy-start
  534.7 62.0 %collective-permute-start.1 = (bf16[127,1024]{1,0:T(8,128)(2,1)S(1)}, bf16[127,1024]{1,0:T(8,128)(2,1)}, u32[]{:S(2)}, u32[]{:S(2)}) collective-permute-start(bf16[127,1024]{1,0:T(8,128)(2,1)S(1)} %slice.58), channel_id=1, source_target_pairs={{0,4},{4,8},{8,12},{12,16},{16,20},{20,24},{24,28},{1,5},{5,9},{9,... | collective-permute-start | bytes 780296 | tf_op jit(solution)/shard_map/ppermute | solution.py:10
  601.2 48.1 %copy-start.1 = (f32[1024]{0:T(1024)S(1)}, f32[1024]{0:T(1024)}, u32[]{:S(2)}) copy-start(f32[1024]{0:T(1024)} %param.12) | copy-start | bytes 12292
Sparse Core Ops, SparseCore 0:
  8.9 25.2 all-gather.3
  35.7 480.3 all-gather.5
  518.2 131.0 all-gather.7
  657.6 42.5 reduce-scatter.1
where the time goes:
time: 709 us
  waiting for transfers between devices  583 us (82%)
  local copies, waits for them, and re-layouts  67.2 us (9%)
  matrix products  29.8 us (4%)
  between operations  13.2 us (2%)
  other arithmetic  7.89 us (1%)
  starting transfers between devices  7.55 us (1%)
    all_gather x1, waiting for transfers between devices, on_device(): weight_rows = lax.all_gather(in_weight, 'ctx', axis=0, tiled=True)  480 us
    reduce_scatter x1, waiting for transfers between devices, on_device(): lax.psum_scatter(terms, 'fsdp', scatter_dimension=1, tiled=True)  42.8 us
    all_gather x1, waiting for transfers between devices, on_device(): lax.all_gather(out_weight, 'ctx', axis=1, tiled=True)  36.2 us
    reshape x1, local copies, waits for them, and re-layouts, toeplitz_blocks(): return tiled[:, :row_count * window].reshape(groups, row_count, window)  34.2 us
    all_gather x1, waiting for transfers between devices, on_device(): whole = lax.all_gather(tokens, 'fsdp', axis=1, tiled=True)  21.4 us
    unnamed x12, local copies, waits for them, and re-layouts  17.1 us
  transfers between devices with their start and end apart: 6, of which 5 were waited for; matrix products, arithmetic and copies ran while one was open for 13% of the time, Pallas kernels for 0%

commit v1 on v0

--- a/solution.py
+++ b/solution.py
@@ -34,7 +34,12 @@
     normed = (values * lax.rsqrt(mean_square + 1e-06) * norm_gain).astype(jnp.bfloat16)
     share = in_weight.shape[2]
     width_all = 3 * share
-    weight_rows = lax.all_gather(in_weight, "ctx", axis=0, tiled=True)
+    ring = [in_weight]
+    for hop in range(7):
+        ring.append(lax.ppermute(ring[-1], "ctx", [(dev, (dev + 1) % 8) for dev in range(8)]))
+    weight_rows = jnp.roll(
+        jnp.concatenate(ring[::-1], axis=0), (lax.axis_index("ctx") + 1) * ring[0].shape[0], axis=0
+    )
     flat_rows = weight_rows.reshape(weight_rows.shape[0], width_all)
     proj = jnp.dot(normed, flat_rows, preferred_element_type=jnp.float32).astype(jnp.bfloat16)
     taps = short_filter.reshape(3, width_all)

time: 709 us -> 835 us (1.18)
  local copies, waits for them, and re-layouts: 67.2 us -> 140 us
  waiting for transfers between devices: 583 us -> 632 us
    ppermute x0 -> x7, waiting for transfers between devices: none -> 589 us  [on_device(): lax.ppermute(ring[-1], 'ctx', [(dev, (dev + 1) % 8) for dev in range(8)])]
    all_gather x1 -> x0, waiting for transfers between devices: 480 us -> none  [on_device(): weight_rows = lax.all_gather(in_weight, 'ctx', axis=0, tiled=True)]
    unnamed x12 -> x41, local copies, waits for them, and re-layouts: 17.1 us -> 66.4 us
    all_gather x1, waiting for transfers between devices: 36.2 us -> 0.01 us  [on_device(): lax.all_gather(out_weight, 'ctx', axis=1, tiled=True)]
    all_gather x1, waiting for transfers between devices: 21.4 us -> 0.01 us  [on_device(): whole = lax.all_gather(tokens, 'fsdp', axis=1, tiled=True)]
    dynamic_slice x0 -> x1, local copies, waits for them, and re-layouts: none -> 21 us  [on_device(): jnp.roll(jnp.concatenate(ring[::-1], axis=0), (lax.axis_index('ctx') + 1)...]
  transfers between devices with their start and end apart: 6 -> 12, of which waited for: 5 -> 9; matrix products, arithmetic and copies ran while one was open for 13% -> 19% of each run, Pallas kernels for 0% -> 0%
where the time goes in v1:
time: 835 us; the launch traced here: 834 us
  waiting for transfers between devices  632 us (76%)
  local copies, waits for them, and re-layouts  140 us (17%)
  matrix products  30.5 us (4%)
  between operations  13.2 us (2%)
  starting transfers between devices  9.35 us (1%)
  other arithmetic  9.29 us (1%)
    ppermute x7, waiting for transfers between devices, on_device(): lax.ppermute(ring[-1], 'ctx', [(dev, (dev + 1) % 8) for dev in range(8)])  589 us
    unnamed x41, local copies, waits for them, and re-layouts  66.4 us
    reduce_scatter x1, waiting for transfers between devices, on_device(): lax.psum_scatter(terms, 'fsdp', scatter_dimension=1, tiled=True)  41.1 us
    reshape x1, local copies, waits for them, and re-layouts, toeplitz_blocks(): return tiled[:, :row_count * window].reshape(groups, row_count, window)  34.2 us
    dynamic_slice x1, local copies, waits for them, and re-layouts, on_device(): jnp.roll(jnp.concatenate(ring[::-1], axis=0), (lax.axis_index('ctx') + 1)...  21 us
  transfers between devices with their start and end apart: 12, of which 9 were waited for; matrix products, arithmetic and copies ran while one was open for 19% of the time, Pallas kernels for 0%

profile of v1, /device:TPU:0, one launch (start us, length us, event | category | flops | bytes accessed | tf_op | source)
XLA Modules:
  0.0 834.4 jit_solution(10037196570881643282)
XLA Ops:
  12.8 71.1 %collective-permute-done = bf16[512,3,1024]{0,2,1:T(8,128)(2,1)S(1)} collective-permute-done((bf16[512,3,1024]{0,2,1:T(8,128)(2,1)S(1)}, bf16[512,3,1024]{0,2,1:T(8,128)(2,1)S(1)}, u32[]{:S(2)}, u32[]{:S(2)}) %collective-permute-start) | collective-permute-done | bytes 3145760 | tf_op jit(solution)/shard_map/ppermute | solution.py:39
  85.5 72.0 %collective-permute-done.1 = bf16[512,3,1024]{0,2,1:T(8,128)(2,1)S(1)} collective-permute-done((bf16[512,3,1024]{0,2,1:T(8,128)(2,1)S(1)}, bf16[512,3,1024]{0,2,1:T(8,128)(2,1)S(1)}, u32[]{:S(2)}, u32[]{:S(2)}) %collective-permute-start.1) | collective-permute-done | bytes 3145760 | tf_op jit(solution)/shard_map/ppermute | solution.py:39
  159.2 71.1 %collective-permute-done.2 = bf16[512,3,1024]{0,2,1:T(8,128)(2,1)S(1)} collective-permute-done((bf16[512,3,1024]{0,2,1:T(8,128)(2,1)S(1)}, bf16[512,3,1024]{0,2,1:T(8,128)(2,1)S(1)}, u32[]{:S(2)}, u32[]{:S(2)}) %collective-permute-start.2) | collective-permute-done | bytes 3145760 | tf_op jit(solution)/shard_map/ppermute | solution.py:39
  232.0 70.4 %collective-permute-done.3 = bf16[512,3,1024]{0,2,1:T(8,128)(2,1)} collective-permute-done((bf16[512,3,1024]{0,2,1:T(8,128)(2,1)S(1)}, bf16[512,3,1024]{0,2,1:T(8,128)(2,1)}, u32[]{:S(2)}, u32[]{:S(2)}) %collective-permute-start.3) | collective-permute-done | bytes 3145760 | tf_op jit(solution)/shard_map/ppermute | solution.py:39
  302.4 69.6 %collective-permute-done.4 = bf16[512,3,1024]{0,2,1:T(8,128)(2,1)} collective-permute-done((bf16[512,3,1024]{0,2,1:T(8,128)(2,1)}, bf16[512,3,1024]{0,2,1:T(8,128)(2,1)}, u32[]{:S(2)}, u32[]{:S(2)}) %collective-permute-start.4) | collective-permute-done | bytes 3145760 | tf_op jit(solution)/shard_map/ppermute | solution.py:39
  372.2 121.6 %collective-permute-done.5 = bf16[512,3,1024]{0,2,1:T(8,128)(2,1)} collective-permute-done((bf16[512,3,1024]{0,2,1:T(8,128)(2,1)}, bf16[512,3,1024]{0,2,1:T(8,128)(2,1)}, u32[]{:S(2)}, u32[]{:S(2)}) %collective-permute-start.5) | collective-permute-done | bytes 3145760 | tf_op jit(solution)/shard_map/ppermute | solution.py:39
  495.8 113.7 %collective-permute-done.6 = bf16[512,3,1024]{0,2,1:T(8,128)(2,1)} collective-permute-done((bf16[512,3,1024]{0,2,1:T(8,128)(2,1)}, bf16[512,3,1024]{0,2,1:T(8,128)(2,1)}, u32[]{:S(2)}, u32[]{:S(2)}) %collective-permute-start.6) | collective-permute-done | bytes 3145760 | tf_op jit(solution)/shard_map/ppermute | solution.py:39
  609.6 3.7 constant_dynamic-update-slice_fusion.15
  613.3 3.7 constant_dynamic-update-slice_fusion.14
  617.0 3.7 constant_dynamic-update-slice_fusion.13
  620.8 3.9 constant_dynamic-update-slice_fusion.12
  634.5 3.8 constant_dynamic-update-slice_fusion.7
  638.3 3.8 constant_dynamic-update-slice_fusion.6
  645.7 3.7 constant_dynamic-update-slice_fusion.4
  657.3 21.0 %constant_dynamic-slice_fusion = bf16[4096,3,1024]{0,2,1:T(8,128)(2,1)} fusion(bf16[8192,3,1024]{0,2,1:T(8,128)(2,1)} %constant_dynamic-update-slice_fusion, s32[]{:T(128)S(6)} %select_n.14), kind=kLoop, calls=%fused_computation.38 | loop fusion | bytes 50331652 | tf_op jit(solution)/shard_map/jit(_roll_dynamic)/dynamic_slice | solution.py:40
  678.3 13.1 %convolution_convert_fusion = bf16[256,3072]{1,0:T(8,128)(2,1)} fusion(bf16[4096,3072]{0,1:T(8,128)(2,1)} %bitcast.13, bf16[256,4096]{1,0:T(8,128)(2,1)S(1)} %copy-done.7, f32[4096]{0:T(1024)S(1)} %copy-done.11, f32[256]{0:T(256)S(1)} %add_rsqrt_fusion), kind=kOutput, calls=%fused_computation.5 | convolution fusion | flops 6447431680 | bytes 28853248 | tf_op jit(solution)/shard_map/dot_general | solution.py:44
  698.7 4.9 collective-permute-start.8
  703.7 5.6 tile.4
  709.3 11.6 %copy.15 = bf16[8,8,256,384]{3,1,2,0:T(8,128)(2,1)S(1)} copy(bf16[8,8,256,384]{3,2,1,0:T(8,128)(2,1)} %bitcast.11) | data formatting | bytes 25165824
  720.9 5.0 slice.59
  726.0 34.2 %reshape.35 = bf16[64,256,383]{2,1,0:T(8,128)(2,1)} reshape(bf16[64,98048]{1,0:T(8,128)(2,1)} %slice.59) | data formatting | bytes 25100288 | tf_op jit(solution)/shard_map/reshape | solution.py:22
  764.7 9.2 %fusion.14 = f32[64,16,256]{2,1,0:T(8,128)} fusion(bf16[383,64,16]{0,2,1:T(8,128)(2,1)} %bitcast.15, bf16[64,256,383]{2,1,0:T(8,128)(2,1)} %reshape.35), kind=kOutput, calls=%fused_computation.40 | convolution fusion | flops 200802304 | bytes 14383104 | tf_op jit(solution)/shard_map/gts,sgc->tgc/dot_general | solution.py:58
  776.5 8.2 fusion.10
  784.7 41.1 %reduce-scatter.2.cloned.1.call-done = f32[256,1024]{1,0:T(8,128)} async-done(((f32[256,4096]{1,0:T(8,128)}), f32[256,1024]{1,0:T(8,128)}) %reduce-scatter.2.cloned.1.call-update) | async-done | bytes 1048592 | tf_op jit(solution)/shard_map/reduce_scatter | solution.py:70
  (69 shorter events, 51.3 us)
Async XLA Ops:
  6.5 487.2 %all-gather.3.cloned.1.call-start = ((), (), s32[]{:S(2)}) async-start(), calls=%async_computation.1 | async-start | bytes 2621440 | tf_op jit(solution)/shard_map/all_gather | solution.py:30
  9.7 74.2 %collective-permute-start = (bf16[512,3,1024]{0,2,1:T(8,128)(2,1)S(1)}, bf16[512,3,1024]{0,2,1:T(8,128)(2,1)S(1)}, u32[]{:S(2)}, u32[]{:S(2)}) collective-permute-start(bf16[512,3,1024]{0,2,1:T(8,128)(2,1)S(1)} %copy.10), channel_id=1, source_target_pairs={{0,4},{4,8},{8,12},{12,16},{16,20},{20,24},{24,28},{28,0},{1,5},{5... | collective-permute-start | bytes 9437192 | tf_op jit(solution)/shard_map/ppermute | solution.py:39
  83.9 1.6 copy-start
  85.5 72.0 %collective-permute-start.1 = (bf16[512,3,1024]{0,2,1:T(8,128)(2,1)S(1)}, bf16[512,3,1024]{0,2,1:T(8,128)(2,1)S(1)}, u32[]{:S(2)}, u32[]{:S(2)}) collective-permute-start(bf16[512,3,1024]{0,2,1:T(8,128)(2,1)S(1)} %collective-permute-done), channel_id=1, source_target_pairs={{0,4},{4,8},{8,12},{12,16},{16,20},{20,24},{24,28},{28,0},{1,5},{5... | collective-permute-start | bytes 9437192 | tf_op jit(solution)/shard_map/ppermute | solution.py:39
  157.5 1.7 copy-start.2
  159.2 71.1 %collective-permute-start.2 = (bf16[512,3,1024]{0,2,1:T(8,128)(2,1)S(1)}, bf16[512,3,1024]{0,2,1:T(8,128)(2,1)S(1)}, u32[]{:S(2)}, u32[]{:S(2)}) collective-permute-start(bf16[512,3,1024]{0,2,1:T(8,128)(2,1)S(1)} %collective-permute-done.1), channel_id=1, source_target_pairs={{0,4},{4,8},{8,12},{12,16},{16,20},{20,24},{24,28},{28,0},{1,5},{5... | collective-permute-start | bytes 9437192 | tf_op jit(solution)/shard_map/ppermute | solution.py:39
  230.3 1.7 copy-start.4
  232.0 70.4 %collective-permute-start.3 = (bf16[512,3,1024]{0,2,1:T(8,128)(2,1)S(1)}, bf16[512,3,1024]{0,2,1:T(8,128)(2,1)}, u32[]{:S(2)}, u32[]{:S(2)}) collective-permute-start(bf16[512,3,1024]{0,2,1:T(8,128)(2,1)S(1)} %collective-permute-done.2), channel_id=1, source_target_pairs={{0,4},{4,8},{8,12},{12,16},{16,20},{20,24},{24,28},{28,0},{1,5},{5... | collective-permute-start | bytes 9437192 | tf_op jit(solution)/shard_map/ppermute | solution.py:39
  302.4 69.7 %collective-permute-start.4 = (bf16[512,3,1024]{0,2,1:T(8,128)(2,1)}, bf16[512,3,1024]{0,2,1:T(8,128)(2,1)}, u32[]{:S(2)}, u32[]{:S(2)}) collective-permute-start(bf16[512,3,1024]{0,2,1:T(8,128)(2,1)} %collective-permute-done.3), channel_id=1, source_target_pairs={{0,4},{4,8},{8,12},{12,16},{16,20},{20,24},{24,28},{28,0},{1,5},{5... | collective-permute-start | bytes 9437192 | tf_op jit(solution)/shard_map/ppermute | solution.py:39
  302.4 474.1 %all-gather.5.cloned.1.call-start = ((), (), s32[]{:S(2)}) async-start(), calls=%async_computation.2 | async-start | bytes 9437184 | tf_op jit(solution)/shard_map/all_gather | solution.py:67
  372.1 121.7 %collective-permute-start.5 = (bf16[512,3,1024]{0,2,1:T(8,128)(2,1)}, bf16[512,3,1024]{0,2,1:T(8,128)(2,1)}, u32[]{:S(2)}, u32[]{:S(2)}) collective-permute-start(bf16[512,3,1024]{0,2,1:T(8,128)(2,1)} %collective-permute-done.4), channel_id=1, source_target_pairs={{0,4},{4,8},{8,12},{12,16},{16,20},{20,24},{24,28},{28,0},{1,5},{5... | collective-permute-start | bytes 9437192 | tf_op jit(solution)/shard_map/ppermute | solution.py:39
  372.1 453.7 %reduce-scatter.2.cloned.1.call-start = ((), (), s32[]{:S(2)}) async-start(), calls=%async_computation.3 | async-start | bytes 5242880 | tf_op jit(solution)/shard_map/reduce_scatter | solution.py:70
  493.7 115.8 %collective-permute-start.6 = (bf16[512,3,1024]{0,2,1:T(8,128)(2,1)}, bf16[512,3,1024]{0,2,1:T(8,128)(2,1)}, u32[]{:S(2)}, u32[]{:S(2)}) collective-permute-start(bf16[512,3,1024]{0,2,1:T(8,128)(2,1)} %collective-permute-done.5), channel_id=1, source_target_pairs={{0,4},{4,8},{8,12},{12,16},{16,20},{20,24},{24,28},{28,0},{1,5},{5... | collective-permute-start | bytes 9437192 | tf_op jit(solution)/shard_map/ppermute | solution.py:39
  620.8 3.9 copy-start.5
  624.7 3.0 copy-start.3
  627.7 3.0 copy-start.1
  657.3 21.0 %copy-start.7 = (bf16[256,4096]{1,0:T(8,128)(2,1)S(1)}, bf16[256,4096]{1,0:T(8,128)(2,1)}, u32[]{:S(2)}) copy-start(bf16[256,4096]{1,0:T(8,128)(2,1)} %all-gather.3.cloned.1.call-done) | copy-start | bytes 6291460
  657.3 21.0 %copy-start.11 = (f32[4096]{0:T(1024)S(1)}, f32[4096]{0:T(1024)}, u32[]{:S(2)}) copy-start(f32[4096]{0:T(1024)} %param.8) | copy-start | bytes 49156
  678.3 15.2 %copy-start.9 = (f32[3,3,1024]{2,1,0:T(4,128)S(1)}, f32[3,3,1024]{2,1,0:T(4,128)}, u32[]{:S(2)}) copy-start(f32[3,3,1024]{2,1,0:T(4,128)} %param.10) | copy-start | bytes 110596
  692.2 2.7 collective-permute-start.7
  696.7 6.9 copy-start.10
  697.8 0.8 copy-start.6
  698.7 61.6 %collective-permute-start.8 = (bf16[127,1024]{1,0:T(8,128)(2,1)S(1)}, bf16[127,1024]{1,0:T(8,128)(2,1)}, u32[]{:S(2)}, u32[]{:S(2)}) collective-permute-start(bf16[127,1024]{1,0:T(8,128)(2,1)S(1)} %slice.58), channel_id=1, source_target_pairs={{0,4},{4,8},{8,12},{12,16},{16,20},{20,24},{24,28},{1,5},{5,9},{9,... | collective-permute-start | bytes 780296 | tf_op jit(solution)/shard_map/ppermute | solution.py:10
  764.7 11.8 %copy-start.8 = (f32[1024]{0:T(1024)S(1)}, f32[1024]{0:T(1024)}, u32[]{:S(2)}) copy-start(f32[1024]{0:T(1024)} %param.12) | copy-start | bytes 12292
Sparse Core Ops, SparseCore 0:
  302.5 23.4 all-gather.2
  372.2 200.9 all-gather.4
  784.9 40.8 reduce-scatter.1
